TPU v7x, 32 devices: a whole 2x2x4 slice. The times are simulated.
32 devices in a mesh: grp: 2 (over y), gx: 4 (over z), gy: 2 (over x), gz: 2 (over core).
Axes of the slice: x: 2, y: 2, z: 4, core: 2. Of those that a mesh axis runs over, the one named last changes fastest.
Arguments:
- alignment_token_ids: int32 [128, 128], P(('grp', 'gx'), ('gy', 'gz')), parts along dimension 0, may hold values from 0 to 22
- homolog_profile: bfloat16 [128, 128, 256], P(('grp', 'gx'), ('gy', 'gz')), parts along dimension 0, may hold values from -6 to 6
- alignment_mask: int32 [128, 128], P(('grp', 'gx'), ('gy', 'gz')), parts along dimension 0, may hold values 0 or 1
- pair_features: bfloat16 [256, 128, 128], P(('grp', 'gy', 'gz'), 'gx'), parts along dimension 0, may hold values from -4 to 6
- symbol_lookup_weights: bfloat16 [23, 256], replicated, may hold values from -6 to 6
- asking_weights: bfloat16 [256, 256], replicated, may hold values from -0.375 to 0.375
- lookup_weights: bfloat16 [256, 256], replicated, may hold values from -0.375 to 0.375
- content_weights: bfloat16 [256, 256], replicated, may hold values from -0.375 to 0.375
- sigmoid_switch_weights: bfloat16 [256, 256], replicated, may hold values from -0.375 to 0.375
- resulting_weights: bfloat16 [256, 256], replicated, may hold values from -0.75 to 0.75
- pair_bias_matrix: float32 [128, 8], replicated, may hold values from -0.9 to 48
- first_factor_weights: bfloat16 [256, 32], replicated, may hold values from -0.375 to 0.375
- second_factor_weights: bfloat16 [256, 32], replicated, may hold values from -0.375 to 0.375
- outer_mixing_weight: bfloat16 [1024, 128], replicated, may hold values from -1 to 1
- widening_weight: bfloat16 [128, 512], replicated, may hold values from -0.5 to 0.5
- narrowing_weight: bfloat16 [512, 128], replicated, may hold values from -0.375 to 0.375
Outputs:
- profile_refreshed: bfloat16 [128, 128, 256], P(('grp', 'gx'), ('gy', 'gz')), parts along dimension 0
- pair_output: bfloat16 [256, 128, 128], P(('grp', 'gy', 'gz'), 'gx'), parts along dimension 0
There are 2 independent parts, one for each index of `grp`. A program takes and returns all parts, laid end to end along the dimension named above; an argument that names none is the same for every part. Nothing has to cross between parts.
All inputs are finite; a program needn't handle non-finite values. No bound on the sum of `alignment_mask` on one device may be relied on, other than what follows from the above.
Results may differ from a plain program's by a relative error of at most 0.013.
Values may be sent and summed in bfloat16 or wider, within the bound.
No kernel may reach another device: no remote copies, remote signals or barrier semaphores. Data moves between devices by JAX's collectives and lax.ppermute only.
A program may use at most 64 MiB of HBM per device.

v0:
```python
import jax
import jax.numpy as jnp
from jax import lax
from jax.sharding import PartitionSpec as P


def standardize_lastaxis(values):
    average = jnp.mean(values, axis=-1, keepdims=True)
    centred = values - average
    return centred * lax.rsqrt(jnp.mean(centred * centred, axis=-1, keepdims=True) + 1e-05)


def attend(state, queries, key_piece, value_piece, valid_piece, bias_rows):
    sequence_total, residue_total, feature_vectors = queries.shape
    piece_len = key_piece.shape[1]
    head_count = bias_rows.shape[1]
    head_size = feature_vectors // head_count
    running_max, running_sum, weighted = state
    scores = jnp.einsum(
        "sihd,sjhd->sihj",
        queries.reshape(sequence_total, residue_total, head_count, head_size),
        key_piece.reshape(sequence_total, piece_len, head_count, head_size),
        preferred_element_type=jnp.float32,
    ) * head_size ** (-0.5)
    scores = (
        scores
        + bias_rows[None]
        + ((valid_piece.astype(jnp.float32) - 1.0) * 1000000000.0)[:, None, None, :]
    )
    new_max = jnp.max(scores, axis=-1)
    rescale = jnp.exp(running_max - new_max)
    exp_scores = jnp.exp(scores - new_max[:, :, :, None])
    new_sum = running_sum * rescale + jnp.sum(exp_scores, axis=-1)
    accumulated = jnp.einsum(
        "sihj,sjhd->sihd",
        exp_scores.astype(jnp.bfloat16),
        value_piece.reshape(sequence_total, piece_len, head_count, head_size),
        preferred_element_type=jnp.float32,
    )
    new_weighted = (
        weighted.reshape(sequence_total, residue_total, head_count, head_size)
        * rescale[:, :, :, None]
        + accumulated
    )
    return (new_max, new_sum, new_weighted.reshape(sequence_total, residue_total, feature_vectors))


def local(
    alignment_token_ids,
    homolog_profile,
    alignment_mask,
    pair_features,
    symbol_lookup_weights,
    asking_weights,
    lookup_weights,
    content_weights,
    sigmoid_switch_weights,
    resulting_weights,
    pair_bias_matrix,
    first_factor_weights,
    second_factor_weights,
    outer_mixing_weight,
    widening_weight,
    narrowing_weight,
):
    sequence_total, residue_total, feature_vectors = homolog_profile.shape
    head_count = pair_bias_matrix.shape[1]
    side_width = first_factor_weights.shape[1]
    pair_width = pair_features.shape[2]
    class_labels = jnp.arange(symbol_lookup_weights.shape[0], dtype=jnp.int32)
    indicator_encoding = (alignment_token_ids[:, :, None] == class_labels).astype(jnp.bfloat16)
    profile_arriving = homolog_profile.astype(jnp.float32) + jnp.einsum(
        "srv,vc->src", indicator_encoding, symbol_lookup_weights, preferred_element_type=jnp.float32
    )
    standardized_profile = standardize_lastaxis(profile_arriving).astype(jnp.bfloat16)
    flat_rows = standardized_profile.reshape(sequence_total * residue_total, feature_vectors)

    def project(row_block, weight, row_total):
        return (
            jnp.dot(row_block, weight, preferred_element_type=jnp.float32)
            .astype(jnp.bfloat16)
            .reshape(sequence_total, row_total, feature_vectors)
        )

    queries = project(flat_rows, asking_weights, residue_total)
    sigmoid_switch = jax.nn.sigmoid(
        jnp.dot(flat_rows, sigmoid_switch_weights, preferred_element_type=jnp.float32)
    ).reshape(sequence_total, residue_total, feature_vectors)
    validity_mask = alignment_mask.astype(jnp.bfloat16)
    pair_normed = standardize_lastaxis(pair_features.astype(jnp.float32))
    bias_local = jnp.einsum(
        "ijc,ch->ihj", pair_normed, pair_bias_matrix, precision=lax.Precision.HIGHEST
    )
    bias_rows = lax.all_gather(bias_local, "gx", axis=2, tiled=True)
    start_state = (
        jnp.full((sequence_total, residue_total, head_count), -jnp.inf, jnp.float32),
        jnp.zeros((sequence_total, residue_total, head_count), jnp.float32),
        jnp.zeros((sequence_total, residue_total, feature_vectors), jnp.float32),
    )
    keys_local = project(flat_rows, lookup_weights, residue_total)
    values_local = project(flat_rows, content_weights, residue_total)
    final_state = attend(
        start_state,
        queries,
        lax.all_gather(keys_local, ("gy", "gz"), axis=1, tiled=True),
        lax.all_gather(values_local, ("gy", "gz"), axis=1, tiled=True),
        lax.all_gather(validity_mask, ("gy", "gz"), axis=1, tiled=True),
        bias_rows,
    )
    softmax_combined = (
        final_state[2].reshape(
            sequence_total, residue_total, head_count, feature_vectors // head_count
        )
        / final_state[1][:, :, :, None]
    )
    switched_result = (
        sigmoid_switch * softmax_combined.reshape(sequence_total, residue_total, feature_vectors)
    ).astype(jnp.bfloat16)
    attention_projector = jnp.dot(
        switched_result.reshape(sequence_total * residue_total, feature_vectors),
        resulting_weights,
        preferred_element_type=jnp.float32,
    )
    profile_refreshed = (
        profile_arriving
        + attention_projector.reshape(sequence_total, residue_total, feature_vectors)
    ).astype(jnp.bfloat16)
    averaged_products = (
        standardize_lastaxis(profile_refreshed.astype(jnp.float32))
        .astype(jnp.bfloat16)
        .reshape(sequence_total * residue_total, feature_vectors)
    )
    mask_floating = alignment_mask.astype(jnp.float32)[:, :, None]
    left_side = (
        (
            jnp.dot(
                averaged_products, first_factor_weights, preferred_element_type=jnp.float32
            ).reshape(sequence_total, residue_total, side_width)
            * mask_floating
        )
        .astype(jnp.bfloat16)
        .reshape(sequence_total, residue_total * side_width)
    )
    right_side = (
        (
            jnp.dot(
                averaged_products, second_factor_weights, preferred_element_type=jnp.float32
            ).reshape(sequence_total, residue_total, side_width)
            * mask_floating
        )
        .astype(jnp.bfloat16)
        .reshape(sequence_total, residue_total * side_width)
    )
    left_all, mask_rows = (
        lax.all_gather(left_side, "gx", axis=0, tiled=True),
        lax.all_gather(validity_mask, "gx", axis=0, tiled=True),
    )
    right_wide, mask_wide = (
        lax.all_gather(right_side, ("gy", "gz"), axis=1, tiled=True),
        lax.all_gather(validity_mask, ("gy", "gz"), axis=1, tiled=True),
    )
    right_cols, mask_cols = (
        lax.all_to_all(right_wide, "gx", split_axis=1, concat_axis=0, tiled=True),
        lax.all_to_all(mask_wide, "gx", split_axis=1, concat_axis=0, tiled=True),
    )
    pair_count = jnp.einsum("si,sj->ij", mask_rows, mask_cols, preferred_element_type=jnp.float32)
    panel_rows = 16

    def outer_panel(panel_index):
        left_rows = lax.dynamic_slice_in_dim(
            left_all, panel_index * (panel_rows * side_width), panel_rows * side_width, 1
        )
        outer_block = jnp.einsum(
            "sa,sb->ab", left_rows, right_cols, preferred_element_type=jnp.float32
        ).astype(jnp.bfloat16)
        outer_block = (
            outer_block.reshape(panel_rows, side_width, residue_total, side_width)
            .transpose(0, 2, 1, 3)
            .reshape(panel_rows * residue_total, side_width * side_width)
        )
        return jnp.dot(
            outer_block, outer_mixing_weight, preferred_element_type=jnp.float32
        ).reshape(panel_rows, residue_total, pair_width)

    mixed_pair = lax.map(
        outer_panel, jnp.arange(residue_total // panel_rows, dtype=jnp.int32)
    ).reshape(residue_total, residue_total, pair_width)
    pair_mid = pair_features.astype(jnp.float32) + mixed_pair / (pair_count[:, :, None] + 1.0)
    trans_rows = (
        standardize_lastaxis(pair_mid)
        .astype(jnp.bfloat16)
        .reshape(residue_total * residue_total, pair_width)
    )
    expanded = jax.nn.relu(
        jnp.dot(trans_rows, widening_weight, preferred_element_type=jnp.float32)
    ).astype(jnp.bfloat16)
    pair_output = (
        pair_mid
        + jnp.dot(expanded, narrowing_weight, preferred_element_type=jnp.float32).reshape(
            residue_total, residue_total, pair_width
        )
    ).astype(jnp.bfloat16)
    return (profile_refreshed, pair_output)


def solution(mesh):
    in_specs = (
        P(("grp", "gx"), ("gy", "gz")),
        P(("grp", "gx"), ("gy", "gz"), None),
        P(("grp", "gx"), ("gy", "gz")),
        P(("grp", "gy", "gz"), "gx", None),
        P(),
        P(),
        P(),
        P(),
        P(),
        P(),
        P(),
        P(),
        P(),
        P(),
        P(),
        P(),
    )
    out_specs = (P(("grp", "gx"), ("gy", "gz"), None), P(("grp", "gy", "gz"), "gx", None))
    return jax.shard_map(local, mesh=mesh, in_specs=in_specs, out_specs=out_specs, check_vma=False)
```

profile of v0, /device:TPU:0, one launch (start us, length us, event | category | flops | bytes accessed | tf_op | source)
XLA Modules:
  0.0 149.4 jit_solution(12472776725563297926)
XLA Ops:
  7.2 0.0 copy-start
  7.2 0.0 all-gather.4.cloned.1.call-start
  7.3 1.5 fusion.43
  8.8 0.3 multiply_reduce_fusion.1
  9.0 0.2 multiply_convert_fusion.1
  9.3 0.9 convolution_convert_fusion.3
  10.2 0.0 all-gather.4.cloned.1.call-update
  10.2 0.6 fusion.42
  10.8 6.2 %all-gather = bf16[4,32,16]{1,2,0:T(8,128)(2,1)S(1)} all-gather(bf16[1,32,16]{1,2,0:T(8,128)(2,1)S(1)} %bitcast.123), channel_id=1, replica_groups=mesh['grp'=2,'gx'=4,'gy'=2,'gz'=2] {'gy','gz'}, dimensions={0}, use_global_device_ids=true | all-gather | bytes 5120 | tf_op jit(solution)/shard_map/all_gather | solution.py:107
  17.1 0.1 reshape.151
  17.2 0.1 all_to_all.32
  17.2 0.7 reshape.161
  17.9 5.3 %all-to-all-start.1 = ((bf16[4,2,256]{2,1,0:T(2,128)(2,1)}), bf16[4,2,256]{2,1,0:T(2,128)(2,1)S(1)}, u32[]{:S(2)}, u32[]{:S(2)}) async-start(bf16[4,2,256]{2,1,0:T(2,128)(2,1)} %reshape.161), calls=%async_computation.1 | async-start | bytes 8192 | tf_op jit(solution)/shard_map/all_to_all | solution.py:164
  23.3 0.9 convolution_convert_fusion.1
  24.2 0.0 all-gather.6.cloned.1.call-update
  24.2 0.2 convert_reduce_fusion
  24.4 0.4 fusion.25
  24.9 2.2 %convolution_bitcast_fusion.1 = f32[32,8,32]{2,1,0:T(8,128)S(1)} fusion(bf16[32,32,128]{2,1,0:T(8,128)(2,1)S(1)} %copy-done.1, f32[32,32]{1,0:T(8,128)S(1)} %add_rsqrt_fusion.1, f32[32,32]{1,0:T(8,128)S(1)} %broadcast_multiply_fusion.1, f32[128,8]{0,1:T(8,128)S(1)} %copy-done.15), kind=kOutput, calls=%fused_computation.31 | convolution fusion | flops 12976128 | bytes 307200 | tf_op jit(solution)/shard_map/ijc,ch->ihj/dot_general | solution.py:91
  27.1 0.1 copy.37
  27.2 0.2 convolution_convert_fusion.2
  27.5 16.1 %all_gather.23 = f32[32,8,128]{0,1,2:T(8,128)S(1)} all-gather(f32[32,8,32]{0,1,2:T(8,128)S(1)} %copy.37), channel_id=1, replica_groups=mesh['grp'=2,'gx'=4,'gy'=2,'gz'=2] {'gx'}, dimensions={2}, use_global_device_ids=true | all-gather | bytes 163840 | tf_op jit(solution)/shard_map/all_gather | solution.py:94
  43.6 1.4 reshape_reshape.3
  45.0 0.2 copy.38
  45.2 13.5 %all_gather.28 = bf16[64,32]{1,0:T(8,128)(2,1)S(1)} all-gather(bf16[16,32]{1,0:T(8,128)(2,1)S(1)} %get-tuple-element.50), channel_id=1, replica_groups=mesh['grp'=2,'gx'=4,'gy'=2,'gz'=2] {'gx'}, dimensions={0}, use_global_device_ids=true | all-gather | bytes 5120 | tf_op jit(solution)/shard_map/all_gather | solution.py:156
  58.7 0.1 reshape.162
  58.8 0.2 convolution_add_fusion.2
  59.0 2.3 %copy.35 = bf16[16,128,256]{1,2,0:T(8,128)(2,1)} copy(bf16[16,128,256]{2,1,0:T(8,128)(2,1)} %all-gather.4.cloned.1.call-done) | data formatting | bytes 2097152 | tf_op jit(solution)/shard_map/all_gather | solution.py:105
  61.3 2.3 %fusion.44 = (f32[16,32,8]{1,2,0:T(8,128)S(1)}, f32[16,32,8,128]{3,1,2,0:T(8,128)S(1)}) fusion(f32[16,128]{1,0:T(8,128)S(1)} %add_multiply_fusion, f32[32,8,128]{2,0,1:T(8,128)S(1)} %copy.38, bf16[16,128,8,32]{1,3,2,0:T(8,128)(2,1)} %bitcast.113, bf16[16,32,8,32]{3,2,1,0:T(8,128)(2,1)} %reshape_reshape.3), kind=kOutput, calls=%fused_computation.79 | convolution fusion | flops 35647488 | bytes 3563520 | tf_op jit(solution)/shard_map/sihd,sjhd->sihj/dot_general | solution.py:19
  63.6 1.3 fusion.6
  64.9 0.0 all-gather.6.cloned.1.call-done
  65.0 2.3 %copy.40 = bf16[16,128,256]{1,2,0:T(8,128)(2,1)} copy(bf16[16,128,256]{2,1,0:T(8,128)(2,1)} %all-gather.6.cloned.1.call-done) | data formatting | bytes 2097152 | tf_op jit(solution)/shard_map/all_gather | solution.py:106
  67.2 3.3 %fusion.4 = f32[16,32,8,32]{1,3,2,0:T(8,128)} fusion(bf16[16,128,8,32]{1,3,2,0:T(8,128)(2,1)} %bitcast.114, f32[16,32,8,128]{3,1,2,0:T(8,128)S(1)} %get-tuple-element.54, f32[16,32,8]{1,2,0:T(8,128)S(1)} %get-tuple-element.48, f32[16,32,8]{1,2,0:T(8,128)S(1)} %get-tuple-element.53, f32[16,32,8]{1,2,0:T(8,128)S(1)} %get-tuple-element.47), kind=kOutput, calls=%fused_computation.7 | convolution fusion | flops 34865152 | bytes 3719168 | tf_op jit(solution)/shard_map/sihj,sjhd->sihd/dot_general | solution.py:34
  70.6 2.0 %copy.41 = f32[16,32,8,32]{3,2,1,0:T(8,128)S(1)} copy(f32[16,32,8,32]{1,3,2,0:T(8,128)} %fusion.4) | data formatting | bytes 1048576 | tf_op jit(solution)/shard_map/div | solution.py:111
  72.6 1.4 reshape.144
  74.0 1.4 fusion.13
  75.4 0.3 convert_reduce_fusion.1
  75.7 0.3 fusion.27
  76.0 0.3 fusion.16
  76.3 0.2 reshape.146
  76.5 5.4 %all_gather.27 = bf16[16,4096]{1,0:T(8,128)(2,1)S(1)} all-gather(bf16[16,1024]{1,0:T(8,128)(2,1)S(1)} %reshape.146), channel_id=1, replica_groups=mesh['grp'=2,'gx'=4,'gy'=2,'gz'=2] {'gy','gz'}, dimensions={1}, use_global_device_ids=true | all-gather | bytes 163840 | tf_op jit(solution)/shard_map/all_gather | solution.py:159
  81.9 0.7 copy.51
  82.6 5.1 %all-to-all-start = ((bf16[16,4,1024]{2,0,1:T(8,128)(2,1)}), bf16[16,4,1024]{2,0,1:T(8,128)(2,1)S(1)}, u32[]{:S(2)}, u32[]{:S(2)}) async-start(bf16[16,4,1024]{2,0,1:T(8,128)(2,1)} %bitcast.93), calls=%async_computation | async-start | bytes 262144 | tf_op jit(solution)/shard_map/all_to_all | solution.py:163
  87.7 0.3 fusion.15
  88.0 0.2 reshape.145
  88.2 14.1 %all_gather.26 = bf16[64,1024]{1,0:T(8,128)(2,1)S(1)} all-gather(bf16[16,1024]{1,0:T(8,128)(2,1)S(1)} %reshape.145), channel_id=1, replica_groups=mesh['grp'=2,'gx'=4,'gy'=2,'gz'=2] {'gx'}, dimensions={0}, use_global_device_ids=true | all-gather | bytes 163840 | tf_op jit(solution)/shard_map/all_gather | solution.py:155
  102.3 37.2 %while.10 = (s32[]{:T(128)}, f32[2,16,32,128]{3,2,1,0:T(8,128)S(1)}, s32[2]{0:T(128)S(1)}, bf16[64,1024]{1,0:T(8,128)(2,1)S(1)}, bf16[64,1024]{1,0:T(8,128)(2,1)...) while((s32[]{:T(128)}, f32[2,16,32,128]{3,2,1,0:T(8,128)S(1)}, ...), condition=%wide.region_9.10_spmd, body=%wide.region_8.9_spmd.sunk | while | flops 201850880 | bytes 9109671 | solution.py:185
  102.4 0.6 dynamic_slice.12
  103.6 0.5 convolution_convert_fusion.5
  104.1 4.4 %reshape.165 = bf16[16,32,32,32]{3,2,1,0:T(8,128)(2,1)} reshape(bf16[512,1024]{1,0:T(8,128)(2,1)S(1)} %convolution_convert_fusion.5) | data formatting | bytes 2097152 | tf_op jit(solution)/shard_map/while/body/eval_jaxpr/reshape | solution.py:177
  108.4 5.9 %copy.54 = bf16[16,32,32,32]{3,2,1,0:T(8,128)(2,1)} copy(bf16[16,32,32,32]{3,1,2,0:T(8,128)(2,1)} %bitcast.107) | data formatting | bytes 2097152 | tf_op jit(solution)/shard_map/while/body/eval_jaxpr/transpose | solution.py:178
  114.3 6.2 %reshape.166 = bf16[16,32,1024]{2,1,0:T(8,128)(2,1)S(1)} reshape(bf16[16,32,32,32]{3,2,1,0:T(8,128)(2,1)} %copy.54) | data formatting | bytes 2097152 | tf_op jit(solution)/shard_map/reshape.62
  120.5 0.4 fusion.72
  121.0 0.6 dynamic_slice.12
  122.2 0.5 convolution_convert_fusion.5
  122.7 4.4 %reshape.165 = bf16[16,32,32,32]{3,2,1,0:T(8,128)(2,1)} reshape(bf16[512,1024]{1,0:T(8,128)(2,1)S(1)} %convolution_convert_fusion.5) | data formatting | bytes 2097152 | tf_op jit(solution)/shard_map/while/body/eval_jaxpr/reshape | solution.py:177
  127.0 5.9 %copy.54 = bf16[16,32,32,32]{3,2,1,0:T(8,128)(2,1)} copy(bf16[16,32,32,32]{3,1,2,0:T(8,128)(2,1)} %bitcast.107) | data formatting | bytes 2097152 | tf_op jit(solution)/shard_map/while/body/eval_jaxpr/transpose | solution.py:178
  133.0 6.2 %reshape.166 = bf16[16,32,1024]{2,1,0:T(8,128)(2,1)S(1)} reshape(bf16[16,32,32,32]{3,2,1,0:T(8,128)(2,1)} %copy.54) | data formatting | bytes 2097152 | tf_op jit(solution)/shard_map/reshape.62
  139.1 0.4 fusion.72
  139.6 0.2 bitcast_divide_fusion
  139.8 0.2 fusion.35
  140.1 0.4 multiply_reduce_fusion
  140.5 0.5 multiply_convert_fusion
  141.0 0.7 fusion.8
  141.6 0.9 add_convert_fusion
  (49 shorter events, 0.2 us)
Async XLA Ops:
  7.2 68.2 %copy-start = (bf16[256,256]{1,0:T(8,128)(2,1)S(1)}, bf16[256,256]{1,0:T(8,128)(2,1)}, u32[]{:S(2)}) copy-start(bf16[256,256]{1,0:T(8,128)(2,1)} %param.27) | copy-start | bytes 393220
  7.2 2.1 %copy-start.5 = (bf16[256,256]{1,0:T(8,128)(2,1)S(1)}, bf16[256,256]{1,0:T(8,128)(2,1)}, u32[]{:S(2)}) copy-start(bf16[256,256]{1,0:T(8,128)(2,1)} %param.24) | copy-start | bytes 393220
  7.2 3.0 %copy-start.8 = (s32[16,32]{1,0:T(8,128)S(1)}, s32[16,32]{1,0:T(8,128)}, u32[]{:S(2)}) copy-start(s32[16,32]{1,0:T(8,128)} %param.20) | copy-start | bytes 6148
  7.2 16.1 %copy-start.6 = (bf16[256,256]{1,0:T(8,128)(2,1)S(1)}, bf16[256,256]{1,0:T(8,128)(2,1)}, u32[]{:S(2)}) copy-start(bf16[256,256]{1,0:T(8,128)(2,1)} %param.25) | copy-start | bytes 393220
  7.2 17.0 %copy-start.1 = (bf16[32,32,128]{2,1,0:T(8,128)(2,1)S(1)}, bf16[32,32,128]{2,1,0:T(8,128)(2,1)}, u32[]{:S(2)}) copy-start(bf16[32,32,128]{2,1,0:T(8,128)(2,1)} %param.21) | copy-start | bytes 786436
  7.2 51.8 %all-gather.4.cloned.1.call-start = ((), (), s32[]{:S(2)}) async-start(), calls=%async_computation.2 | async-start | bytes 1310720 | tf_op jit(solution)/shard_map/all_gather | solution.py:105
  8.7 16.1 %copy-start.15 = (f32[128,8]{0,1:T(8,128)S(1)}, f32[128,8]{0,1:T(8,128)}, u32[]{:S(2)}) copy-start(f32[128,8]{0,1:T(8,128)} %param.28) | copy-start | bytes 12292
  9.0 18.2 %copy-start.7 = (bf16[256,256]{1,0:T(8,128)(2,1)S(1)}, bf16[256,256]{1,0:T(8,128)(2,1)}, u32[]{:S(2)}) copy-start(bf16[256,256]{1,0:T(8,128)(2,1)} %param.23) | copy-start | bytes 393220
  17.9 40.8 %all-to-all-start.1 = ((bf16[4,2,256]{2,1,0:T(2,128)(2,1)}), bf16[4,2,256]{2,1,0:T(2,128)(2,1)S(1)}, u32[]{:S(2)}, u32[]{:S(2)}) async-start(bf16[4,2,256]{2,1,0:T(2,128)(2,1)} %reshape.161), calls=%async_computation.1 | async-start | bytes 8192 | tf_op jit(solution)/shard_map/all_to_all | solution.py:164
  23.3 41.7 %all-gather.6.cloned.1.call-start = ((), (), s32[]{:S(2)}) async-start(), calls=%async_computation.3 | async-start | bytes 1310720 | tf_op jit(solution)/shard_map/all_gather | solution.py:106
  72.6 1.4 copy-start.10
  74.0 2.0 %copy-start.9 = (f32[16,32]{1,0:T(8,128)S(1)}, f32[16,32]{1,0:T(8,128)}, u32[]{:S(2)}) copy-start(f32[16,32]{1,0:T(8,128)} %get-tuple-element.49) | copy-start | bytes 6148
  74.0 2.0 %copy-start.13 = (bf16[256,32]{0,1:T(8,128)(2,1)S(1)}, bf16[256,32]{0,1:T(8,128)(2,1)}, u32[]{:S(2)}) copy-start(bf16[256,32]{0,1:T(8,128)(2,1)} %param.30) | copy-start | bytes 49156
  75.3 12.4 %copy-start.14 = (bf16[256,32]{0,1:T(8,128)(2,1)S(1)}, bf16[256,32]{0,1:T(8,128)(2,1)}, u32[]{:S(2)}) copy-start(bf16[256,32]{0,1:T(8,128)(2,1)} %param.29) | copy-start | bytes 49156
  75.3 27.0 %copy-start.2 = (bf16[1024,128]{1,0:T(8,128)(2,1)S(1)}, bf16[1024,128]{1,0:T(8,128)(2,1)}, u32[]{:S(2)}) copy-start(bf16[1024,128]{1,0:T(8,128)(2,1)} %param.31) | copy-start | bytes 786436
  75.4 27.0 %copy-start.3 = (f32[2,16,32,128]{3,2,1,0:T(8,128)S(1)}, f32[2,16,32,128]{3,2,1,0:T(8,128)}, u32[]{:S(2)}) copy-start(f32[2,16,32,128]{3,2,1,0:T(8,128)} %custom-call) | copy-start | bytes 1572868
  75.7 26.6 %copy-start.4 = (bf16[16,32,256]{2,1,0:T(8,128)(2,1)}, bf16[16,32,256]{2,1,0:T(8,128)(2,1)S(1)}, u32[]{:S(2)}) copy-start(bf16[16,32,256]{2,1,0:T(8,128)(2,1)S(1)} %get-tuple-element.56) | copy-start | bytes 786436
  82.6 19.7 %all-to-all-start = ((bf16[16,4,1024]{2,0,1:T(8,128)(2,1)}), bf16[16,4,1024]{2,0,1:T(8,128)(2,1)S(1)}, u32[]{:S(2)}, u32[]{:S(2)}) async-start(bf16[16,4,1024]{2,0,1:T(8,128)(2,1)} %bitcast.93), calls=%async_computation | async-start | bytes 262144 | tf_op jit(solution)/shard_map/all_to_all | solution.py:163
  139.6 1.3 copy-start.11
  139.6 1.3 copy-start.12
Sparse Core Ops, SparseCore 0:
  10.3 19.4 all-gather.3
  31.9 16.7 all-gather.5
where the time goes:
time: 150 us; the launch traced here: 149 us
  blocking collectives  55.4 us (37%)
  local copies, waits for them, and re-layouts  45.8 us (31%)
  matrix products  16.4 us (11%)
  between operations  14.5 us (10%)
  starting transfers between devices  10.4 us (7%)
  other arithmetic  5.47 us (4%)
    all_gather x1, blocking collectives, local(): bias_rows = lax.all_gather(bias_local, 'gx', axis=2, tiled=True)  16.1 us
    all_gather x1, blocking collectives, local(): lax.all_gather(left_side, 'gx', axis=0, tiled=True)  14.1 us
    all_gather x1, blocking collectives, local(): lax.all_gather(validity_mask, 'gx', axis=0, tiled=True)  13.5 us
    another operation x2, local copies, waits for them, and re-layouts  12.3 us
    transpose x2, local copies, waits for them, and re-layouts, outer_panel(): outer_block = outer_block.reshape(panel_rows, side_width, residue_total,...  11.8 us
    reshape x2, local copies, waits for them, and re-layouts, outer_panel(): outer_block.reshape(panel_rows, side_width, residue_total, side_width)  8.7 us
    all_gather x1, blocking collectives, local(): lax.all_gather(validity_mask, ('gy', 'gz'), axis=1, tiled=True)  6.22 us
    all_gather x1, blocking collectives, local(): lax.all_gather(right_side, ('gy', 'gz'), axis=1, tiled=True)  5.42 us
  transfers between devices with their start and end apart: 4, of which 0 were waited for; matrix products, arithmetic and copies ran while one was open for 9% of the time, Pallas kernels for 0%

commit v1 on v0

--- a/solution.py
+++ b/solution.py
@@ -91,7 +91,12 @@
     bias_local = jnp.einsum(
         "ijc,ch->ihj", pair_normed, pair_bias_matrix, precision=lax.Precision.HIGHEST
     )
-    bias_rows = lax.all_gather(bias_local, "gx", axis=2, tiled=True)
+    ring = [bias_local]
+    for hop in range(3):
+        ring.append(lax.ppermute(ring[-1], "gx", [(dev, (dev + 1) % 4) for dev in range(4)]))
+    bias_rows = jnp.roll(
+        jnp.concatenate(ring[::-1], axis=2), (lax.axis_index("gx") + 1) * ring[0].shape[2], axis=2
+    )
     start_state = (
         jnp.full((sequence_total, residue_total, head_count), -jnp.inf, jnp.float32),
         jnp.zeros((sequence_total, residue_total, head_count), jnp.float32),

time: 150 us -> 142 us (0.947)
  blocking collectives: 55.4 us -> 38 us
  waiting for transfers between devices: 0.06 us -> 6.59 us
  starting transfers between devices: 10.4 us -> 12.5 us
    all_gather x1 -> x0, blocking collectives: 16.1 us -> none  [local(): bias_rows = lax.all_gather(bias_local, 'gx', axis=2, tiled=True)]
    ppermute x0 -> x3, waiting for transfers between devices: none -> 6.53 us  [local(): lax.ppermute(ring[-1], 'gx', [(dev, (dev + 1) % 4) for dev in range(4)])]
    ppermute x0 -> x3, starting transfers between devices: none -> 5.26 us  [local(): lax.ppermute(ring[-1], 'gx', [(dev, (dev + 1) % 4) for dev in range(4)])]
    all_to_all x1, starting transfers between devices: 5.09 us -> 3.33 us  [local(): lax.all_to_all(right_wide, 'gx', split_axis=1, concat_axis=0, tiled=True)]
  transfers between devices with their start and end apart: 4 -> 7, of which waited for: 0 -> 1; matrix products, arithmetic and copies ran while one was open for 9% -> 10% of each run, Pallas kernels for 0% -> 0%
where the time goes in v1:
time: 142 us; the launch traced here: 141 us
  local copies, waits for them, and re-layouts  45.8 us (32%)
  blocking collectives  38 us (27%)
  matrix products  16.4 us (12%)
  between operations  14.5 us (10%)
  starting transfers between devices  12.5 us (9%)
  waiting for transfers between devices  6.59 us (5%)
  other arithmetic  5.57 us (4%)
    all_gather x1, blocking collectives, local(): lax.all_gather(left_side, 'gx', axis=0, tiled=True)  14.2 us
    all_gather x1, blocking collectives, local(): lax.all_gather(validity_mask, 'gx', axis=0, tiled=True)  13.2 us
    another operation x2, local copies, waits for them, and re-layouts  12.3 us
    transpose x2, local copies, waits for them, and re-layouts, outer_panel(): outer_block = outer_block.reshape(panel_rows, side_width, residue_total,...  11.8 us
    reshape x2, local copies, waits for them, and re-layouts, outer_panel(): outer_block.reshape(panel_rows, side_width, residue_total, side_width)  8.7 us
    ppermute x3, waiting for transfers between devices, local(): lax.ppermute(ring[-1], 'gx', [(dev, (dev + 1) % 4) for dev in range(4)])  6.53 us
    all_gather x1, blocking collectives, local(): lax.all_gather(right_side, ('gy', 'gz'), axis=1, tiled=True)  5.42 us
    ppermute x3, starting transfers between devices, local(): lax.ppermute(ring[-1], 'gx', [(dev, (dev + 1) % 4) for dev in range(4)])  5.26 us
  transfers between devices with their start and end apart: 7, of which 1 were waited for; matrix products, arithmetic and copies ran while one was open for 10% of the time, Pallas kernels for 0%

profile of v1, /device:TPU:0, one launch (start us, length us, event | category | flops | bytes accessed | tf_op | source)
XLA Modules:
  0.0 140.8 jit_solution(3309407348946778165)
XLA Ops:
  7.2 0.0 all-gather.4.cloned.1.call-start
  7.3 1.5 %fusion.49 = (f32[16,32]{1,0:T(8,128)S(1)}, f32[16,32,256]{2,1,0:T(8,128)S(1)}) fusion(bf16[23,256]{1,0:T(8,128)(2,1)} %param.22, s32[16,32]{1,0:T(8,128)} %param.18, bf16[16,32,256]{2,1,0:T(8,128)(2,1)} %param.19), kind=kOutput, calls=%fused_computation.85 | convolution fusion | flops 6433792 | bytes 802304 | tf_op jit(solution)/shard_map/srv,vc->src/dot_general | solution.py:72
  8.8 0.3 multiply_reduce_fusion.1
  9.0 0.2 multiply_convert_fusion.1
  9.3 0.9 convolution_convert_fusion.3
  10.2 0.2 convert_reduce_fusion
  10.5 0.4 fusion.30
  10.9 2.2 %convolution_bitcast_fusion.1 = f32[32,8,32]{2,1,0:T(8,128)S(1)} fusion(bf16[32,32,128]{2,1,0:T(8,128)(2,1)S(1)} %copy-done.1, f32[32,32]{1,0:T(8,128)S(1)} %add_rsqrt_fusion.1, f32[32,32]{1,0:T(8,128)S(1)} %broadcast_multiply_fusion.1, f32[128,8]{0,1:T(8,128)S(1)} %copy-done.14), kind=kOutput, calls=%fused_computation.32 | convolution fusion | flops 12976128 | bytes 307200 | tf_op jit(solution)/shard_map/ijc,ch->ihj/dot_general | solution.py:91
  13.1 3.1 %collective-permute-start = (f32[32,8,32]{2,1,0:T(8,128)S(1)}, f32[32,8,32]{2,1,0:T(8,128)S(1)}, u32[]{:S(2)}, u32[]{:S(2)}) collective-permute-start(f32[32,8,32]{2,1,0:T(8,128)S(1)} %convolution_bitcast_fusion.1), channel_id=1, source_target_pairs={{0,4},{4,8},{8,12},{12,0},{1,5},{5,9},{9,13},{13,1},{2,6},{6,10},{... | collective-permute-start | bytes 98312 | tf_op jit(solution)/shard_map/ppermute | solution.py:96
  16.2 5.2 %all-gather = bf16[4,32,16]{1,2,0:T(8,128)(2,1)S(1)} all-gather(bf16[1,32,16]{1,2,0:T(8,128)(2,1)S(1)} %bitcast.130), channel_id=1, replica_groups=mesh['grp'=2,'gx'=4,'gy'=2,'gz'=2] {'gy','gz'}, dimensions={0}, use_global_device_ids=true | all-gather | bytes 5120 | tf_op jit(solution)/shard_map/all_gather | solution.py:112
  21.4 0.1 reshape.151
  21.5 0.1 all_to_all.32
  21.5 0.7 reshape.161
  22.2 3.9 %all-to-all-start.1 = ((bf16[4,2,256]{2,1,0:T(2,128)(2,1)}), bf16[4,2,256]{2,1,0:T(2,128)(2,1)S(1)}, u32[]{:S(2)}, u32[]{:S(2)}) async-start(bf16[4,2,256]{2,1,0:T(2,128)(2,1)} %reshape.161), calls=%async_computation.1 | async-start | bytes 8192 | tf_op jit(solution)/shard_map/all_to_all | solution.py:169
  26.1 0.9 convolution_convert_fusion.1
  27.0 0.2 convolution_convert_fusion.2
  27.3 2.1 %collective-permute-start.1 = (f32[32,8,32]{2,1,0:T(8,128)S(1)}, f32[32,8,32]{2,1,0:T(8,128)S(1)}, u32[]{:S(2)}, u32[]{:S(2)}) collective-permute-start(f32[32,8,32]{2,1,0:T(8,128)S(1)} %collective-permute-done), channel_id=1, source_target_pairs={{0,4},{4,8},{8,12},{12,0},{1,5},{5,9},{9,13},{13,1},{2,6},{6,10},{... | collective-permute-start | bytes 98312 | tf_op jit(solution)/shard_map/ppermute | solution.py:96
  29.4 1.4 %reshape_reshape.3 = bf16[16,32,8,32]{3,2,1,0:T(8,128)(2,1)} reshape(bf16[512,256]{1,0:T(8,128)(2,1)S(1)} %convolution_convert_fusion.2) | data formatting | bytes 524288 | tf_op jit(solution)/shard_map/reshape;reshape | solution.py:21
  30.8 13.2 %all_gather.24 = bf16[64,32]{1,0:T(8,128)(2,1)S(1)} all-gather(bf16[16,32]{1,0:T(8,128)(2,1)S(1)} %get-tuple-element.50), channel_id=1, replica_groups=mesh['grp'=2,'gx'=4,'gy'=2,'gz'=2] {'gx'}, dimensions={0}, use_global_device_ids=true | all-gather | bytes 5120 | tf_op jit(solution)/shard_map/all_gather | solution.py:161
  44.0 0.1 reshape.162
  44.1 0.1 collective-permute-start.2
  44.2 0.2 convolution_add_fusion.2
  44.4 6.5 %collective-permute-done.2 = f32[32,8,32]{2,1,0:T(8,128)S(1)} collective-permute-done((f32[32,8,32]{2,1,0:T(8,128)S(1)}, f32[32,8,32]{2,1,0:T(8,128)S(1)}, u32[]{:S(2)}, u32[]{:S(2)}) %collective-permute-start.2) | collective-permute-done | bytes 32800 | tf_op jit(solution)/shard_map/ppermute | solution.py:96
  50.9 0.3 concatenate.6
  51.2 0.1 constant_dynamic-slice_fusion
  51.4 0.0 all-gather.4.cloned.1.call-done
  51.4 2.3 %copy.35 = bf16[16,128,256]{1,2,0:T(8,128)(2,1)} copy(bf16[16,128,256]{2,1,0:T(8,128)(2,1)} %all-gather.4.cloned.1.call-done) | data formatting | bytes 2097152 | tf_op jit(solution)/shard_map/all_gather | solution.py:110
  53.6 2.3 %fusion.9 = (f32[16,32,8]{1,2,0:T(8,128)S(1)}, f32[16,8,128,32]{2,3,1,0:T(8,128)S(1)}) fusion(f32[16,128]{1,0:T(8,128)S(1)} %add_multiply_fusion, f32[32,8,128]{2,0,1:T(8,128)S(1)} %copy.37, bf16[16,128,8,32]{1,3,2,0:T(8,128)(2,1)} %bitcast.120, bf16[16,32,8,32]{3,2,1,0:T(8,128)(2,1)} %reshape_reshape.3), kind=kOutput, calls=%fused_computation.15 | convolution fusion | flops 35647488 | bytes 3563520 | tf_op jit(solution)/shard_map/sihd,sjhd->sihj/dot_general | solution.py:19
  56.0 1.4 fusion.6
  57.3 0.7 exponential_multiply_fusion
  58.0 2.3 %copy.39 = bf16[16,128,256]{1,2,0:T(8,128)(2,1)} copy(bf16[16,128,256]{2,1,0:T(8,128)(2,1)} %all-gather.6.cloned.1.call-done) | data formatting | bytes 2097152 | tf_op jit(solution)/shard_map/all_gather | solution.py:111
  60.3 3.4 %fusion.4 = f32[16,32,8,32]{1,3,2,0:T(8,128)} fusion(bf16[16,128,8,32]{1,3,2,0:T(8,128)(2,1)} %bitcast.121, f32[16,8,128,32]{2,3,1,0:T(8,128)S(1)} %get-tuple-element.54, f32[16,32,8]{1,2,0:T(8,128)} %get-tuple-element.48, f32[16,32,8]{1,2,0:T(8,128)S(1)} %get-tuple-element.53, f32[16,32,8]{1,2,0:T(8,128)} %get-tuple-element.47, ...), kind=kOutput, calls=%fused_computation.7 | convolution fusion | flops 36438016 | bytes 3858432 | tf_op jit(solution)/shard_map/sihj,sjhd->sihd/dot_general | solution.py:34
  63.6 2.0 %copy.40 = f32[16,32,8,32]{3,2,1,0:T(8,128)S(1)} copy(f32[16,32,8,32]{1,3,2,0:T(8,128)} %fusion.4) | data formatting | bytes 1048576 | tf_op jit(solution)/shard_map/div | solution.py:116
  65.7 1.4 reshape.144
  67.1 1.4 fusion.14
  68.5 0.3 convert_reduce_fusion.1
  68.8 0.3 fusion.32
  69.1 0.3 fusion.17
  69.4 0.2 reshape.146
  69.6 5.4 %all_gather.23 = bf16[16,4096]{1,0:T(8,128)(2,1)S(1)} all-gather(bf16[16,1024]{1,0:T(8,128)(2,1)S(1)} %reshape.146), channel_id=1, replica_groups=mesh['grp'=2,'gx'=4,'gy'=2,'gz'=2] {'gy','gz'}, dimensions={1}, use_global_device_ids=true | all-gather | bytes 163840 | tf_op jit(solution)/shard_map/all_gather | solution.py:164
  75.0 0.7 copy.50
  75.7 3.3 %all-to-all-start = ((bf16[16,4,1024]{2,0,1:T(8,128)(2,1)}), bf16[16,4,1024]{2,0,1:T(8,128)(2,1)S(1)}, u32[]{:S(2)}, u32[]{:S(2)}) async-start(bf16[16,4,1024]{2,0,1:T(8,128)(2,1)} %bitcast.100), calls=%async_computation | async-start | bytes 262144 | tf_op jit(solution)/shard_map/all_to_all | solution.py:168
  79.0 0.3 fusion.16
  79.4 0.2 reshape.145
  79.5 14.2 %all_gather.22 = bf16[64,1024]{1,0:T(8,128)(2,1)S(1)} all-gather(bf16[16,1024]{1,0:T(8,128)(2,1)S(1)} %reshape.145), channel_id=1, replica_groups=mesh['grp'=2,'gx'=4,'gy'=2,'gz'=2] {'gx'}, dimensions={0}, use_global_device_ids=true | all-gather | bytes 163840 | tf_op jit(solution)/shard_map/all_gather | solution.py:160
  93.8 37.2 %while.10 = (s32[]{:T(128)}, f32[2,16,32,128]{3,2,1,0:T(8,128)S(1)}, s32[2]{0:T(128)S(1)}, bf16[64,1024]{1,0:T(8,128)(2,1)S(1)}, bf16[64,1024]{1,0:T(8,128)(2,1)...) while((s32[]{:T(128)}, f32[2,16,32,128]{3,2,1,0:T(8,128)S(1)}, ...), condition=%wide.region_9.10_spmd, body=%wide.region_8.9_spmd.sunk | while | flops 201850880 | bytes 9109671 | solution.py:190
  93.8 0.6 dynamic_slice.18
  95.1 0.5 convolution_convert_fusion.5
  95.5 4.3 %reshape.165 = bf16[16,32,32,32]{3,2,1,0:T(8,128)(2,1)} reshape(bf16[512,1024]{1,0:T(8,128)(2,1)S(1)} %convolution_convert_fusion.5) | data formatting | bytes 2097152 | tf_op jit(solution)/shard_map/while/body/eval_jaxpr/reshape | solution.py:182
  99.9 5.9 %copy.53 = bf16[16,32,32,32]{3,2,1,0:T(8,128)(2,1)} copy(bf16[16,32,32,32]{3,1,2,0:T(8,128)(2,1)} %bitcast.114) | data formatting | bytes 2097152 | tf_op jit(solution)/shard_map/while/body/eval_jaxpr/transpose | solution.py:183
  105.8 6.2 %reshape.166 = bf16[16,32,1024]{2,1,0:T(8,128)(2,1)S(1)} reshape(bf16[16,32,32,32]{3,2,1,0:T(8,128)(2,1)} %copy.53) | data formatting | bytes 2097152 | tf_op jit(solution)/shard_map/reshape.62
  111.9 0.4 fusion.77
  112.4 0.6 dynamic_slice.18
  113.7 0.5 convolution_convert_fusion.5
  114.1 4.3 %reshape.165 = bf16[16,32,32,32]{3,2,1,0:T(8,128)(2,1)} reshape(bf16[512,1024]{1,0:T(8,128)(2,1)S(1)} %convolution_convert_fusion.5) | data formatting | bytes 2097152 | tf_op jit(solution)/shard_map/while/body/eval_jaxpr/reshape | solution.py:182
  118.5 5.9 %copy.53 = bf16[16,32,32,32]{3,2,1,0:T(8,128)(2,1)} copy(bf16[16,32,32,32]{3,1,2,0:T(8,128)(2,1)} %bitcast.114) | data formatting | bytes 2097152 | tf_op jit(solution)/shard_map/while/body/eval_jaxpr/transpose | solution.py:183
  124.4 6.2 %reshape.166 = bf16[16,32,1024]{2,1,0:T(8,128)(2,1)S(1)} reshape(bf16[16,32,32,32]{3,2,1,0:T(8,128)(2,1)} %copy.53) | data formatting | bytes 2097152 | tf_op jit(solution)/shard_map/reshape.62
  130.6 0.4 fusion.77
  131.0 0.2 bitcast_divide_fusion
  131.2 0.2 fusion.40
  131.5 0.4 multiply_reduce_fusion
  131.9 0.5 multiply_convert_fusion
  132.4 0.7 fusion.8
  133.1 0.9 add_convert_fusion
  (53 shorter events, 0.2 us)
Async XLA Ops:
  7.2 61.3 %copy-start = (bf16[256,256]{1,0:T(8,128)(2,1)S(1)}, bf16[256,256]{1,0:T(8,128)(2,1)}, u32[]{:S(2)}) copy-start(bf16[256,256]{1,0:T(8,128)(2,1)} %param.27) | copy-start | bytes 393220
  7.2 2.1 %copy-start.5 = (bf16[256,256]{1,0:T(8,128)(2,1)S(1)}, bf16[256,256]{1,0:T(8,128)(2,1)}, u32[]{:S(2)}) copy-start(bf16[256,256]{1,0:T(8,128)(2,1)} %param.24) | copy-start | bytes 393220
  7.2 3.0 %copy-start.1 = (bf16[32,32,128]{2,1,0:T(8,128)(2,1)S(1)}, bf16[32,32,128]{2,1,0:T(8,128)(2,1)}, u32[]{:S(2)}) copy-start(bf16[32,32,128]{2,1,0:T(8,128)(2,1)} %param.21) | copy-start | bytes 786436
  7.2 3.7 %copy-start.14 = (f32[128,8]{0,1:T(8,128)S(1)}, f32[128,8]{0,1:T(8,128)}, u32[]{:S(2)}) copy-start(f32[128,8]{0,1:T(8,128)} %param.28) | copy-start | bytes 12292
  7.2 8.9 %copy-start.8 = (s32[16,32]{1,0:T(8,128)S(1)}, s32[16,32]{1,0:T(8,128)}, u32[]{:S(2)}) copy-start(s32[16,32]{1,0:T(8,128)} %param.20) | copy-start | bytes 6148
  7.2 18.9 %copy-start.6 = (bf16[256,256]{1,0:T(8,128)(2,1)S(1)}, bf16[256,256]{1,0:T(8,128)(2,1)}, u32[]{:S(2)}) copy-start(bf16[256,256]{1,0:T(8,128)(2,1)} %param.25) | copy-start | bytes 393220
  7.2 44.1 %all-gather.4.cloned.1.call-start = ((), (), s32[]{:S(2)}) async-start(), calls=%async_computation.2 | async-start | bytes 1310720 | tf_op jit(solution)/shard_map/all_gather | solution.py:110
  9.0 18.0 %copy-start.7 = (bf16[256,256]{1,0:T(8,128)(2,1)S(1)}, bf16[256,256]{1,0:T(8,128)(2,1)}, u32[]{:S(2)}) copy-start(bf16[256,256]{1,0:T(8,128)(2,1)} %param.23) | copy-start | bytes 393220
  13.1 14.2 %collective-permute-start = (f32[32,8,32]{2,1,0:T(8,128)S(1)}, f32[32,8,32]{2,1,0:T(8,128)S(1)}, u32[]{:S(2)}, u32[]{:S(2)}) collective-permute-start(f32[32,8,32]{2,1,0:T(8,128)S(1)} %convolution_bitcast_fusion.1), channel_id=1, source_target_pairs={{0,4},{4,8},{8,12},{12,0},{1,5},{5,9},{9,13},{13,1},{2,6},{6,10},{... | collective-permute-start | bytes 98312 | tf_op jit(solution)/shard_map/ppermute | solution.py:96
  22.2 21.8 %all-to-all-start.1 = ((bf16[4,2,256]{2,1,0:T(2,128)(2,1)}), bf16[4,2,256]{2,1,0:T(2,128)(2,1)S(1)}, u32[]{:S(2)}, u32[]{:S(2)}) async-start(bf16[4,2,256]{2,1,0:T(2,128)(2,1)} %reshape.161), calls=%async_computation.1 | async-start | bytes 8192 | tf_op jit(solution)/shard_map/all_to_all | solution.py:169
  26.1 31.9 %all-gather.6.cloned.1.call-start = ((), (), s32[]{:S(2)}) async-start(), calls=%async_computation.3 | async-start | bytes 1310720 | tf_op jit(solution)/shard_map/all_gather | solution.py:111
  27.3 16.8 %collective-permute-start.1 = (f32[32,8,32]{2,1,0:T(8,128)S(1)}, f32[32,8,32]{2,1,0:T(8,128)S(1)}, u32[]{:S(2)}, u32[]{:S(2)}) collective-permute-start(f32[32,8,32]{2,1,0:T(8,128)S(1)} %collective-permute-done), channel_id=1, source_target_pairs={{0,4},{4,8},{8,12},{12,0},{1,5},{5,9},{9,13},{13,1},{2,6},{6,10},{... | collective-permute-start | bytes 98312 | tf_op jit(solution)/shard_map/ppermute | solution.py:96
  44.1 6.8 %collective-permute-start.2 = (f32[32,8,32]{2,1,0:T(8,128)S(1)}, f32[32,8,32]{2,1,0:T(8,128)S(1)}, u32[]{:S(2)}, u32[]{:S(2)}) collective-permute-start(f32[32,8,32]{2,1,0:T(8,128)S(1)} %collective-permute-done.1), channel_id=1, source_target_pairs={{0,4},{4,8},{8,12},{12,0},{1,5},{5,9},{9,13},{13,1},{2,6},{6,10},{... | collective-permute-start | bytes 98312 | tf_op jit(solution)/shard_map/ppermute | solution.py:96
  65.6 1.4 copy-start.9
  67.1 2.0 %copy-start.12 = (bf16[256,32]{0,1:T(8,128)(2,1)S(1)}, bf16[256,32]{0,1:T(8,128)(2,1)}, u32[]{:S(2)}) copy-start(bf16[256,32]{0,1:T(8,128)(2,1)} %param.30) | copy-start | bytes 49156
  68.4 10.6 %copy-start.13 = (bf16[256,32]{0,1:T(8,128)(2,1)S(1)}, bf16[256,32]{0,1:T(8,128)(2,1)}, u32[]{:S(2)}) copy-start(bf16[256,32]{0,1:T(8,128)(2,1)} %param.29) | copy-start | bytes 49156
  68.4 25.3 %copy-start.2 = (bf16[1024,128]{1,0:T(8,128)(2,1)S(1)}, bf16[1024,128]{1,0:T(8,128)(2,1)}, u32[]{:S(2)}) copy-start(bf16[1024,128]{1,0:T(8,128)(2,1)} %param.31) | copy-start | bytes 786436
  68.4 25.3 %copy-start.3 = (f32[2,16,32,128]{3,2,1,0:T(8,128)S(1)}, f32[2,16,32,128]{3,2,1,0:T(8,128)}, u32[]{:S(2)}) copy-start(f32[2,16,32,128]{3,2,1,0:T(8,128)} %custom-call) | copy-start | bytes 1572868
  68.8 25.0 %copy-start.4 = (bf16[16,32,256]{2,1,0:T(8,128)(2,1)}, bf16[16,32,256]{2,1,0:T(8,128)(2,1)S(1)}, u32[]{:S(2)}) copy-start(bf16[16,32,256]{2,1,0:T(8,128)(2,1)S(1)} %get-tuple-element.56) | copy-start | bytes 786436
  75.7 18.1 %all-to-all-start = ((bf16[16,4,1024]{2,0,1:T(8,128)(2,1)}), bf16[16,4,1024]{2,0,1:T(8,128)(2,1)S(1)}, u32[]{:S(2)}, u32[]{:S(2)}) async-start(bf16[16,4,1024]{2,0,1:T(8,128)(2,1)} %bitcast.100), calls=%async_computation | async-start | bytes 262144 | tf_op jit(solution)/shard_map/all_to_all | solution.py:168
  131.0 1.3 copy-start.10
  131.0 1.3 copy-start.11
Sparse Core Ops, SparseCore 0:
  10.3 19.4 all-gather.3
  31.9 16.6 all-gather.5
